TPU v7x, 256 devices: a whole 4x4x8 slice. The times are simulated.
256 devices in a mesh: dp: 4 (over y), expert: 64 (over x, z, core).
Axes of the slice: x: 4, y: 4, z: 8, core: 2. Of those that a mesh axis runs over, the one named last changes fastest.
Arguments:
- tokens: bfloat16 [6144, 4096], P(('dp', 'expert')), may hold values from -6 to 6
- out_grad: bfloat16 [6144, 4096], P(('dp', 'expert')), may hold values from -6 to 6
- routes: int32 [6144, 8], P(('dp', 'expert')), may hold values from 0 to 63, all different within a row; in each aligned block of 24 rows (0 to 23, 24 to 47, ...) at most 4 rows name the same one
- gates: bfloat16 [6144, 8], P(('dp', 'expert')), may hold values from 0.099609375 to 0.5
- w_gate: bfloat16 [64, 768, 4096], P('expert', 'dp'), may hold values from -0.09375 to 0.09375
- w_up: bfloat16 [64, 768, 4096], P('expert', 'dp'), may hold values from -0.09375 to 0.09375
- w_down: bfloat16 [64, 768, 4096], P('expert', 'dp'), may hold values from -0.21875 to 0.21875
Outputs:
- d_tokens: bfloat16 [6144, 4096], P(('dp', 'expert'))
- d_gate: bfloat16 [64, 768, 4096], P('expert', 'dp')
- d_up: bfloat16 [64, 768, 4096], P('expert', 'dp')
- d_down: bfloat16 [64, 768, 4096], P('expert', 'dp')
Inputs may be any that keep to these rules, and one draw needn't show every extreme that they name: `routes`: each row names 8 different experts. Within the 24 rows of one device no expert is named by more than 4 rows, and in every draw some expert is named by exactly 4 rows of some device.
All inputs are finite; a program needn't handle non-finite values.
Results may differ from a plain program's by a relative error of at most 0.015.
Values may be sent and summed in bfloat16 or wider, within the bound.
A program may use at most 128 MiB of HBM per device.

v0:
```python
from functools import partial
import jax
import jax.numpy as jnp
from jax import lax
from jax.sharding import PartitionSpec as P


def cell_match(routes, experts, capacity):
    expert_ids = jnp.arange(experts, dtype=jnp.int32)
    onehot = (routes[:, :, None] == expert_ids).astype(jnp.int32)
    chosen = jnp.sum(onehot, axis=1)
    earlier = jnp.cumsum(chosen, axis=0) - chosen
    slot_index = jnp.sum(onehot * earlier[:, None, :], axis=2)
    target = routes * capacity + slot_index
    cell_ids = jnp.arange(experts * capacity, dtype=jnp.int32)
    return target[:, :, None] == cell_ids


def placement(matches, experts, capacity):
    return jnp.any(matches, axis=1).reshape(-1, experts, capacity).astype(jnp.bfloat16)


def weighting(matches, gates, experts, capacity):
    spread = jnp.where(matches, gates.astype(jnp.float32)[:, :, None], 0.0)
    return jnp.sum(spread, axis=1).reshape(-1, experts, capacity)


def per_device(tokens, out_grad, routes, gates, w_gate, w_up, w_down):
    tok_rows, features = tokens.shape
    top_count = routes.shape[1]
    experts = lax.axis_size("expert")
    groups = lax.axis_size("dp")
    capacity = max(2, min(tok_rows, 3 * tok_rows * top_count // (2 * experts)))
    match_fn = partial(cell_match, experts=experts, capacity=capacity)
    place_fn = partial(placement, experts=experts, capacity=capacity)
    weight_fn = partial(weighting, experts=experts, capacity=capacity)
    own_match = match_fn(routes)
    own_place = place_fn(own_match)
    own_weight = weight_fn(own_match, gates)
    input_send = jnp.einsum(
        "tec,td->ecd", own_place, tokens, preferred_element_type=jnp.float32
    ).astype(jnp.bfloat16)
    grad_send = jnp.einsum(
        "tec,td->ecd", own_weight, out_grad.astype(jnp.float32), precision=lax.Precision.HIGHEST
    ).astype(jnp.bfloat16)
    input_recv, grad_recv = (
        lax.all_to_all(input_send, "expert", split_axis=0, concat_axis=0, tiled=True),
        lax.all_to_all(grad_send, "expert", split_axis=0, concat_axis=0, tiled=True),
    )
    input_recv = input_recv.reshape(experts, 1, capacity, features)
    grad_recv = grad_recv.reshape(experts, 1, capacity, features)
    input_slots, grad_slots = (
        lax.all_gather(input_recv, "dp", axis=1, tiled=True),
        lax.all_gather(grad_recv, "dp", axis=1, tiled=True),
    )
    input_rows = input_slots.reshape(-1, features)
    grad_rows = grad_slots.reshape(-1, features)
    gate_w = w_gate[0]
    up_w = w_up[0]
    down_w = w_down[0]
    gate_pre = jnp.einsum("rd,fd->rf", input_rows, gate_w, preferred_element_type=jnp.float32)
    up_pre = jnp.einsum("rd,fd->rf", input_rows, up_w, preferred_element_type=jnp.float32)
    sigmoid_gate = jax.nn.sigmoid(gate_pre)
    silu_gate = gate_pre * sigmoid_gate
    hidden = (silu_gate * up_pre).astype(jnp.bfloat16)
    d_hidden = jnp.einsum("rd,fd->rf", grad_rows, down_w, preferred_element_type=jnp.float32)
    d_up_act = (d_hidden * silu_gate).astype(jnp.bfloat16)
    d_gate_act = (
        d_hidden * up_pre * sigmoid_gate * (1.0 + gate_pre * (1.0 - sigmoid_gate))
    ).astype(jnp.bfloat16)
    grad_down = jnp.einsum(
        "rf,rd->fd", hidden, grad_rows, preferred_element_type=jnp.float32
    ).astype(jnp.bfloat16)
    grad_gate = jnp.einsum(
        "rf,rd->fd", d_gate_act, input_rows, preferred_element_type=jnp.float32
    ).astype(jnp.bfloat16)
    grad_up = jnp.einsum(
        "rf,rd->fd", d_up_act, input_rows, preferred_element_type=jnp.float32
    ).astype(jnp.bfloat16)
    partial_sum = jnp.einsum("rf,fd->rd", d_gate_act, gate_w, preferred_element_type=jnp.float32)
    partial_sum = partial_sum + jnp.einsum(
        "rf,fd->rd", d_up_act, up_w, preferred_element_type=jnp.float32
    )
    rounded = partial_sum.astype(jnp.bfloat16).reshape(experts, groups, capacity, features)
    held = lax.optimization_barrier(rounded).astype(jnp.float32)
    slot_total = lax.psum_scatter(
        held.astype(jnp.bfloat16), "dp", scatter_dimension=1, tiled=True
    ).astype(jnp.float32)
    returned = lax.all_to_all(
        slot_total[:, 0].astype(jnp.bfloat16), "expert", split_axis=0, concat_axis=0, tiled=True
    ).astype(jnp.float32)
    summed = jnp.einsum(
        "tec,ecd->td", own_place.astype(jnp.float32), returned, precision=lax.Precision.HIGHEST
    )
    return (summed.astype(jnp.bfloat16), grad_gate[None], grad_up[None], grad_down[None])


def solution(mesh):
    in_specs = (
        P(("dp", "expert"), None),
        P(("dp", "expert"), None),
        P(("dp", "expert"), None),
        P(("dp", "expert"), None),
        P("expert", "dp", None),
        P("expert", "dp", None),
        P("expert", "dp", None),
    )
    out_specs = (
        P(("dp", "expert"), None),
        P("expert", "dp", None),
        P("expert", "dp", None),
        P("expert", "dp", None),
    )
    return jax.shard_map(
        per_device, mesh=mesh, in_specs=in_specs, out_specs=out_specs, check_vma=False
    )
```

profile of v0, /device:TPU:1, one launch (start us, length us, event | category | flops | bytes accessed | tf_op | source)
XLA Modules:
  0.0 475.0 jit_solution(9894178153079241439)
XLA Ops:
  7.2 0.0 copy-start
  7.2 0.0 all-gather.7.cloned.1.call-start
  7.2 0.9 copy.53
  8.1 0.1 convert_reduce_fusion
  8.3 0.5 select_reduce_fusion.1
  8.8 0.1 fusion.17
  9.0 0.1 copy.55
  9.1 0.1 copy.68
  9.2 1.7 convolution_convert_fusion
  10.9 1.6 copy.63
  12.5 64.0 %all_to_all.15 = bf16[64,4,4096]{2,1,0:T(4,128)(2,1)S(1)} all-to-all(bf16[64,4,4096]{2,1,0:T(4,128)(2,1)S(1)} %copy.63), channel_id=1, replica_groups=mesh['dp'=4,'expert'=64] {'expert'}, dimensions={0} | all-to-all | bytes 4194304 | tf_op jit(solution)/shard_map/all_to_all | solution.py:47
  76.6 2.5 copy.64
  79.1 0.0 all-gather.7.cloned.1.call-update
  79.1 0.0 all-gather.5.cloned.1.call-start
  79.1 0.6 copy-done.7
  79.7 0.1 copy.56
  79.8 0.1 select_reduce_fusion
  80.0 0.1 copy.57
  80.1 1.8 convolution_convert_fusion.1
  81.9 1.6 copy.59
  83.5 56.9 %all_to_all.16 = bf16[64,4,4096]{2,1,0:T(4,128)(2,1)S(1)} all-to-all(bf16[64,4,4096]{2,1,0:T(4,128)(2,1)S(1)} %copy.59), channel_id=1, replica_groups=mesh['dp'=4,'expert'=64] {'expert'}, dimensions={0} | all-to-all | bytes 4194304 | tf_op jit(solution)/shard_map/all_to_all | solution.py:48
  140.3 2.5 copy.60
  142.8 0.0 all-gather.5.cloned.1.call-update
  142.9 0.2 reduce-scatter.2.cloned.1.call-start
  143.1 18.4 %all-gather.7.cloned.1.call-done = bf16[64,16,4096]{2,0,1:T(8,128)(2,1)} async-done(((bf16[64,4,4096]{2,0,1:T(8,128)(2,1)}), bf16[64,16,4096]{2,0,1:T(8,128)(2,1)}) %all-gather.7.cloned.1.call-update) | async-done | bytes 8388624 | tf_op jit(solution)/shard_map/all_gather | solution.py:53
  161.5 11.2 %copy.65 = bf16[64,16,4096]{2,1,0:T(8,128)(2,1)} copy(bf16[64,16,4096]{2,0,1:T(8,128)(2,1)} %all-gather.7.cloned.1.call-done) | data formatting | bytes 16777216 | tf_op jit(solution)/shard_map/all_gather | solution.py:53
  172.8 7.5 %fusion.7 = f32[1024,192]{0,1:T(8,128)} fusion(bf16[1024,4096]{1,0:T(8,128)(2,1)} %bitcast.48, bf16[1,192,4096]{2,1,0:T(8,128)(2,1)S(1)} %copy-done), kind=kOutput, calls=%fused_computation.14 | convolution fusion | flops 1610612736 | bytes 10747904 | tf_op jit(solution)/shard_map/rd,fd->rf/dot_general | solution.py:61
  180.3 0.0 copy-done.2
  180.3 0.0 copy-done.3
  180.3 3.8 fusion.10
  184.2 65.9 %all-gather.5.cloned.1.call-done = bf16[64,16,4096]{2,0,1:T(8,128)(2,1)} async-done(((bf16[64,4,4096]{2,0,1:T(8,128)(2,1)}), bf16[64,16,4096]{2,0,1:T(8,128)(2,1)}) %all-gather.5.cloned.1.call-update) | async-done | bytes 8388624 | tf_op jit(solution)/shard_map/all_gather | solution.py:54
  250.1 11.6 %copy.61 = bf16[64,16,4096]{2,1,0:T(8,128)(2,1)} copy(bf16[64,16,4096]{2,0,1:T(8,128)(2,1)} %all-gather.5.cloned.1.call-done) | data formatting | bytes 16777216 | tf_op jit(solution)/shard_map/all_gather | solution.py:54
  261.6 0.0 copy-done.9
  261.6 6.4 %multiply_convert_fusion.1 = (bf16[1024,192]{0,1:T(8,128)(2,1)S(1)}, bf16[1024,192]{0,1:T(8,128)(2,1)S(1)}) fusion(f32[1024,192]{0,1:T(8,128)S(1)} %copy-done.9, f32[1024,192]{0,1:T(8,128)S(1)} %copy-done.11, bf16[1024,4096]{1,0:T(8,128)(2,1)} %bitcast.52, bf16[1,192,4096]{2,1,0:T(8,128)(2,1)S(1)} %copy-done.8), kind=kOutput, calls=%fused_computation.22 | convolution fusion | flops 1613168640 | bytes 12320768 | tf_op jit(solution)/shard_map/rd,fd->rf/dot_general | solution.py:66
  268.1 0.0 copy-start.4
  268.1 8.1 %fusion.5 = f32[1024,4096]{1,0:T(8,128)} fusion(bf16[1024,192]{0,1:T(8,128)(2,1)S(1)} %get-tuple-element.5, bf16[1,192,4096]{2,1,0:T(8,128)(2,1)S(1)} %copy-done), kind=kOutput, calls=%fused_computation.12 | convolution fusion | flops 1610612736 | bytes 18743296 | tf_op jit(solution)/shard_map/rf,fd->rd/dot_general | solution.py:80
  276.2 11.4 %add_convert_fusion = bf16[1024,4096]{1,0:T(8,128)(2,1)} fusion(f32[1024,4096]{1,0:T(8,128)} %fusion.5, bf16[1024,192]{0,1:T(8,128)(2,1)S(1)} %get-tuple-element.4, bf16[1,192,4096]{2,1,0:T(8,128)(2,1)S(1)} %copy-done.3), kind=kOutput, calls=%fused_computation | convolution fusion | flops 1619001344 | bytes 27131904 | tf_op jit(solution)/shard_map/rf,fd->rd/dot_general | solution.py:81
  287.6 13.3 %reshape.48 = bf16[64,4,4,4096]{3,2,1,0:T(4,128)(2,1)} reshape(bf16[1024,4096]{1,0:T(8,128)(2,1)} %add_convert_fusion) | data formatting | bytes 16777216 | tf_op jit(solution)/shard_map/reshape | solution.py:84
  300.9 11.2 %copy.66 = bf16[64,4,4,4096]{3,0,2,1:T(8,128)(2,1)} copy(bf16[64,4,4,4096]{3,2,1,0:T(4,128)(2,1)} %reshape.48) | data formatting | bytes 16777216 | tf_op jit(solution)/shard_map/optimization_barrier | solution.py:85
  312.1 0.0 reduce-scatter.2.cloned.1.call-update
  312.1 84.3 %reduce-scatter.2.cloned.1.call-done = bf16[64,1,4,4096]{3,0,2,1:T(8,128)(2,1)} async-done(((bf16[64,4,4,4096]{3,0,2,1:T(8,128)(2,1)}), bf16[64,1,4,4096]{3,0,2,1:T(8,128)(2,1)}) %reduce-scatter.2.cloned.1.call-update) | async-done | bytes 2097168 | tf_op jit(solution)/shard_map/reduce_scatter | solution.py:86
  396.4 4.6 copy.67
  401.0 11.4 %all-to-all-start.2 = ((bf16[64,4,4096]{2,1,0:T(4,128)(2,1)}), bf16[64,4,4096]{2,1,0:T(4,128)(2,1)}, u32[]{:S(2)}, u32[]{:S(2)}) async-start(bf16[64,4,4096]{2,1,0:T(4,128)(2,1)} %copy.67), calls=%async_computation.3 | async-start | bytes 4194304 | tf_op jit(solution)/shard_map/all_to_all | solution.py:89
  412.4 6.3 %fusion.1 = bf16[1,192,4096]{2,1,0:T(8,128)(2,1)} fusion(bf16[1024,192]{0,1:T(8,128)(2,1)S(1)} %copy-done.5, bf16[1024,4096]{1,0:T(8,128)(2,1)} %bitcast.49), kind=kOutput, calls=%fused_computation.7 | convolution fusion | flops 1611399168 | bytes 10354688 | tf_op jit(solution)/shard_map/rf,rd->fd/dot_general | solution.py:77
  418.7 6.4 %fusion = bf16[1,192,4096]{2,1,0:T(8,128)(2,1)} fusion(bf16[1024,192]{0,1:T(8,128)(2,1)S(1)} %get-tuple-element.5, bf16[1024,4096]{1,0:T(8,128)(2,1)} %bitcast.50), kind=kOutput, calls=%fused_computation.6 | convolution fusion | flops 1611399168 | bytes 10354688 | tf_op jit(solution)/shard_map/rf,rd->fd/dot_general | solution.py:74
  425.2 6.5 %fusion.2 = bf16[1,192,4096]{2,1,0:T(8,128)(2,1)} fusion(bf16[1024,4096]{1,0:T(8,128)(2,1)} %bitcast.53, f32[1024,192]{0,1:T(8,128)S(1)} %copy-done.12, f32[1024,192]{0,1:T(8,128)S(1)} %copy-done.10), kind=kOutput, calls=%fused_computation.8 | convolution fusion | flops 1612578816 | bytes 11534336 | tf_op jit(solution)/shard_map/rf,rd->fd/dot_general | solution.py:71
  431.7 31.7 %all-to-all-done.2 = bf16[64,4,4096]{2,1,0:T(4,128)(2,1)} async-done(((bf16[64,4,4096]{2,1,0:T(4,128)(2,1)}), bf16[64,4,4096]{2,1,0:T(4,128)(2,1)}, u32[]{:S(2)}, u32[]{:S(2)}) %all-to-all-start.2) | async-done | bytes 2097184 | tf_op jit(solution)/shard_map/all_to_all | solution.py:89
  463.4 4.6 fusion.3
  (23 shorter events, 0.1 us)
Async XLA Ops:
  7.2 165.6 %copy-start = (bf16[1,192,4096]{2,1,0:T(8,128)(2,1)S(1)}, bf16[1,192,4096]{2,1,0:T(8,128)(2,1)}, u32[]{:S(2)}) copy-start(bf16[1,192,4096]{2,1,0:T(8,128)(2,1)} %param.11) | copy-start | bytes 4718596
  7.2 154.4 %all-gather.7.cloned.1.call-start = ((), (), s32[]{:S(2)}) async-start(), calls=%async_computation.6 | async-start | bytes 10485760 | tf_op jit(solution)/shard_map/all_gather | solution.py:53
  79.1 0.7 copy-start.7
  79.1 1.0 copy-start.6
  79.1 171.0 %all-gather.5.cloned.1.call-start = ((), (), s32[]{:S(2)}) async-start(), calls=%async_computation.5 | async-start | bytes 10485760 | tf_op jit(solution)/shard_map/all_gather | solution.py:54
  142.9 253.6 %reduce-scatter.2.cloned.1.call-start = ((), (), s32[]{:S(2)}) async-start(), calls=%async_computation.4 | async-start | bytes 10485760 | tf_op jit(solution)/shard_map/reduce_scatter | solution.py:86
  172.8 7.5 %copy-start.2 = (bf16[64,16,4096]{2,1,0:T(8,128)(2,1)S(1)}, bf16[64,16,4096]{2,1,0:T(8,128)(2,1)}, u32[]{:S(2)}) copy-start(bf16[64,16,4096]{2,1,0:T(8,128)(2,1)} %copy.65) | copy-start | bytes 25165828
  172.8 7.6 %copy-start.3 = (bf16[1,192,4096]{2,1,0:T(8,128)(2,1)S(1)}, bf16[1,192,4096]{2,1,0:T(8,128)(2,1)}, u32[]{:S(2)}) copy-start(bf16[1,192,4096]{2,1,0:T(8,128)(2,1)} %param.12) | copy-start | bytes 4718596
  250.1 11.6 %copy-start.8 = (bf16[1,192,4096]{2,1,0:T(8,128)(2,1)S(1)}, bf16[1,192,4096]{2,1,0:T(8,128)(2,1)}, u32[]{:S(2)}) copy-start(bf16[1,192,4096]{2,1,0:T(8,128)(2,1)} %param.13) | copy-start | bytes 4718596
  250.1 11.6 %copy-start.9 = (f32[1024,192]{0,1:T(8,128)S(1)}, f32[1024,192]{0,1:T(8,128)}, u32[]{:S(2)}) copy-start(f32[1024,192]{0,1:T(8,128)} %fusion.7) | copy-start | bytes 2359300
  250.1 11.6 %copy-start.11 = (f32[1024,192]{0,1:T(8,128)S(1)}, f32[1024,192]{0,1:T(8,128)}, u32[]{:S(2)}) copy-start(f32[1024,192]{0,1:T(8,128)} %fusion.10) | copy-start | bytes 2359300
  268.1 8.1 %copy-start.4 = (bf16[1024,192]{0,1:T(8,128)(2,1)}, bf16[1024,192]{0,1:T(8,128)(2,1)S(1)}, u32[]{:S(2)}) copy-start(bf16[1024,192]{0,1:T(8,128)(2,1)S(1)} %get-tuple-element.4) | copy-start | bytes 1179652
  401.0 11.4 %copy-start.5 = (bf16[1024,192]{0,1:T(8,128)(2,1)S(1)}, bf16[1024,192]{0,1:T(8,128)(2,1)}, u32[]{:S(2)}) copy-start(bf16[1024,192]{0,1:T(8,128)(2,1)} %copy-done.4) | copy-start | bytes 1179652
  401.0 62.4 %all-to-all-start.2 = ((bf16[64,4,4096]{2,1,0:T(4,128)(2,1)}), bf16[64,4,4096]{2,1,0:T(4,128)(2,1)}, u32[]{:S(2)}, u32[]{:S(2)}) async-start(bf16[64,4,4096]{2,1,0:T(4,128)(2,1)} %copy.67), calls=%async_computation.3 | async-start | bytes 4194304 | tf_op jit(solution)/shard_map/all_to_all | solution.py:89
  418.7 6.5 %copy-start.10 = (f32[1024,192]{0,1:T(8,128)S(1)}, f32[1024,192]{0,1:T(8,128)}, u32[]{:S(2)}) copy-start(f32[1024,192]{0,1:T(8,128)} %fusion.7) | copy-start | bytes 2359300
  418.7 6.5 %copy-start.12 = (f32[1024,192]{0,1:T(8,128)S(1)}, f32[1024,192]{0,1:T(8,128)}, u32[]{:S(2)}) copy-start(f32[1024,192]{0,1:T(8,128)} %fusion.10) | copy-start | bytes 2359300
  425.2 42.8 %copy-start.1 = (bf16[1,192,4096]{2,1,0:T(8,128)(2,1)S(1)}, bf16[1,192,4096]{2,1,0:T(8,128)(2,1)}, u32[]{:S(2)}) copy-start(bf16[1,192,4096]{2,1,0:T(8,128)(2,1)} %param.11) | copy-start | bytes 4718596
Sparse Core Ops, SparseCore 0:
  79.2 82.2 all-gather.6
  163.4 86.6 all-gather.4
  312.3 84.1 reduce-scatter.1
where the time goes:
time: 484 us; the launch traced here: 475 us
  waiting for transfers between devices  200 us (41%)
  blocking collectives  121 us (25%)
  matrix products  64.6 us (13%)
  local copies, waits for them, and re-layouts  62.1 us (13%)
  between operations  14.4 us (3%)
  starting transfers between devices  11.7 us (2%)
    reduce_scatter x1, waiting for transfers between devices, per_device(): lax.psum_scatter(held.astype(jnp.bfloat16), 'dp', scatter_dimension=1, ti...  84.3 us
    all_gather x1, waiting for transfers between devices, per_device(): lax.all_gather(grad_recv, 'dp', axis=1, tiled=True)  65.9 us
    all_to_all x1, blocking collectives, per_device(): lax.all_to_all(input_send, 'expert', split_axis=0, concat_axis=0, tiled=T...  64 us
    all_to_all x1, blocking collectives, per_device(): lax.all_to_all(grad_send, 'expert', split_axis=0, concat_axis=0, tiled=True)  56.9 us
    all_to_all x1, waiting for transfers between devices, per_device(): lax.all_to_all(slot_total[:, 0].astype(jnp.bfloat16), 'expert', split_axi...  31.7 us
    all_gather x1, waiting for transfers between devices, per_device(): lax.all_gather(input_recv, 'dp', axis=1, tiled=True)  18.4 us
    reshape x1, local copies, waits for them, and re-layouts, per_device(): partial_sum.astype(jnp.bfloat16)  13.3 us
    all_gather x1, local copies, waits for them, and re-layouts, per_device(): lax.all_gather(grad_recv, 'dp', axis=1, tiled=True)  11.6 us
  transfers between devices with their start and end apart: 4, of which 4 were waited for; matrix products, arithmetic and copies ran while one was open for 10% of the time, Pallas kernels for 0%

commit v1 on v0

--- a/solution.py
+++ b/solution.py
@@ -1,8 +1,18 @@
+import functools
 from functools import partial
 import jax
 import jax.numpy as jnp
 from jax import lax
 from jax.sharding import PartitionSpec as P
+from jax.lax import all_to_all, axis_size
+
+
+def wrap_sample_by_axis(mat, along_dim):
+    local_part = all_to_all(jnp.stack([mat] * axis_size("dp")), "dp", 0, 0)
+    return jnp.concatenate(local_part, axis=along_dim)
+
+
+_test_sums_all = functools.partial(wrap_sample_by_axis, along_dim=1)
 
 
 def cell_match(routes, experts, capacity):
@@ -50,7 +60,7 @@
     input_recv = input_recv.reshape(experts, 1, capacity, features)
     grad_recv = grad_recv.reshape(experts, 1, capacity, features)
     input_slots, grad_slots = (
-        lax.all_gather(input_recv, "dp", axis=1, tiled=True),
+        _test_sums_all(input_recv),
         lax.all_gather(grad_recv, "dp", axis=1, tiled=True),
     )
     input_rows = input_slots.reshape(-1, features)

time: 484 us -> 516 us (1.066)
  blocking collectives: 121 us -> 223 us
  waiting for transfers between devices: 200 us -> 119 us
  local copies, waits for them, and re-layouts: 62.1 us -> 76.5 us
    all_to_all x0 -> x1, blocking collectives: none -> 102 us  [wrap_sample_by_axis(): local_part = all_to_all(jnp.stack([mat] * axis_size('dp')), 'dp', 0, 0)]
    all_gather x1, waiting for transfers between devices: 65.9 us -> 0.01 us  [per_device(): lax.all_gather(grad_recv, 'dp', axis=1, tiled=True)]
    another operation x0 -> x2, local copies, waits for them, and re-layouts: none -> 21.9 us  [the longest x1 12.5 us: per_device(): input_rows = input_slots.reshape(-1, features)]
    all_gather x1 -> x0, waiting for transfers between devices: 18.4 us -> none  [per_device(): lax.all_gather(input_recv, 'dp', axis=1, tiled=True)]
    all_gather x1 -> x0, local copies, waits for them, and re-layouts: 11.2 us -> none  [per_device(): lax.all_gather(input_recv, 'dp', axis=1, tiled=True)]
    all_to_all x1, blocking collectives: 56.9 us -> 64 us  [per_device(): lax.all_to_all(grad_send, 'expert', split_axis=0, concat_axis=0, tiled=True)]
    all_to_all x1, blocking collectives: 64 us -> 57.2 us  [per_device(): lax.all_to_all(input_send, 'expert', split_axis=0, concat_axis=0, tiled=T...]
    reshape x0 -> x1, local copies, waits for them, and re-layouts: none -> 6.17 us  [wrap_sample_by_axis(): return jnp.concatenate(local_part, axis=along_dim)]
  transfers between devices with their start and end apart: 4 -> 3, of which waited for: 4 -> 2; matrix products, arithmetic and copies ran while one was open for 10% -> 11% of each run, Pallas kernels for 0% -> 0%
where the time goes in v1:
time: 516 us; the launch traced here: 507 us
  blocking collectives  223 us (43%)
  waiting for transfers between devices  119 us (23%)
  local copies, waits for them, and re-layouts  76.5 us (15%)
  matrix products  61.2 us (12%)
  between operations  14.6 us (3%)
  starting transfers between devices  11.4 us (2%)
    all_to_all x1, blocking collectives, wrap_sample_by_axis(): local_part = all_to_all(jnp.stack([mat] * axis_size('dp')), 'dp', 0, 0)  102 us
    reduce_scatter x1, waiting for transfers between devices, per_device(): lax.psum_scatter(held.astype(jnp.bfloat16), 'dp', scatter_dimension=1, ti...  84.4 us
    all_to_all x1, blocking collectives, per_device(): lax.all_to_all(grad_send, 'expert', split_axis=0, concat_axis=0, tiled=True)  64 us
    all_to_all x1, blocking collectives, per_device(): lax.all_to_all(input_send, 'expert', split_axis=0, concat_axis=0, tiled=T...  57.2 us
    all_to_all x1, waiting for transfers between devices, per_device(): lax.all_to_all(slot_total[:, 0].astype(jnp.bfloat16), 'expert', split_axi...  35 us
    reshape x1, local copies, waits for them, and re-layouts, per_device(): partial_sum.astype(jnp.bfloat16)  13.1 us
    another operation x1, local copies, waits for them, and re-layouts, per_device(): input_rows = input_slots.reshape(-1, features)  12.5 us
    dot_general x1, matrix products, per_device(): jnp.einsum('rf,fd->rd', d_up_act, up_w, preferred_element_type=jnp.float32)  11.4 us
  transfers between devices with their start and end apart: 3, of which 2 were waited for; matrix products, arithmetic and copies ran while one was open for 11% of the time, Pallas kernels for 0%

profile of v1, /device:TPU:1, one launch (start us, length us, event | category | flops | bytes accessed | tf_op | source)
XLA Modules:
  0.0 507.5 jit_solution(4563966732281106380)
XLA Ops:
  7.2 0.0 copy-start
  7.2 0.0 all-gather.3.cloned.1.call-start
  7.2 0.9 copy.52
  8.1 0.1 convert_reduce_fusion
  8.3 0.5 select_reduce_fusion.1
  8.8 0.8 copy.55
  9.6 0.1 select_reduce_fusion
  9.7 0.1 copy.56
  9.8 2.7 convolution_convert_fusion.1
  12.5 1.6 copy.58
  14.2 64.0 %all_to_all.20 = bf16[64,4,4096]{2,1,0:T(4,128)(2,1)S(1)} all-to-all(bf16[64,4,4096]{2,1,0:T(4,128)(2,1)S(1)} %copy.58), channel_id=1, replica_groups=mesh['dp'=4,'expert'=64] {'expert'}, dimensions={0} | all-to-all | bytes 4194304 | tf_op jit(solution)/shard_map/all_to_all | solution.py:58
  78.2 2.5 copy.59
  80.7 0.0 all-gather.3.cloned.1.call-update
  80.7 0.0 reduce-scatter.2.cloned.1.call-start
  80.8 0.1 fusion.17
  80.9 0.1 copy.54
  81.1 0.1 copy.66
  81.2 0.5 copy-done.6
  81.6 0.7 convolution_convert_fusion
  82.4 1.6 copy.62
  84.0 57.2 %all_to_all.21 = bf16[64,4,4096]{2,1,0:T(4,128)(2,1)} all-to-all(bf16[64,4,4096]{2,1,0:T(4,128)(2,1)S(1)} %copy.62), channel_id=1, replica_groups=mesh['dp'=4,'expert'=64] {'expert'}, dimensions={0} | all-to-all | bytes 4194304 | tf_op jit(solution)/shard_map/all_to_all | solution.py:57
  141.2 9.4 %stack.3 = bf16[4,64,1,4,4096]{4,3,1,2,0:T(4,128)(2,1)} broadcast(bf16[64,4,4096]{2,1,0:T(4,128)(2,1)} %all_to_all.21), dimensions={1,3,4} | broadcast | bytes 10485760 | tf_op jit(solution)/shard_map/stack | solution.py:11
  150.6 102.0 %all_to_all.22 = bf16[4,64,1,4,4096]{4,3,1,2,0:T(4,128)(2,1)S(1)} all-to-all(bf16[4,64,1,4,4096]{4,3,1,2,0:T(4,128)(2,1)} %stack.3), channel_id=1, replica_groups=mesh['dp'=4,'expert'=64] {'dp'}, dimensions={0} | all-to-all | bytes 16777216 | tf_op jit(solution)/shard_map/all_to_all | solution.py:11
  252.6 6.2 %copy.63 = bf16[64,4,1,4,4096]{4,3,1,0,2:T(4,128)(2,1)} copy(bf16[64,4,1,4,4096]{4,3,0,2,1:T(4,128)(2,1)S(1)} %bitcast.50) | data formatting | bytes 16777216 | tf_op jit(solution)/shard_map/reshape | solution.py:12
  258.8 12.5 %reshape_reshape.3 = bf16[1024,4096]{1,0:T(8,128)(2,1)} reshape(bf16[64,4,1,4,4096]{4,3,1,0,2:T(4,128)(2,1)} %copy.63) | data formatting | bytes 16777216 | tf_op jit(solution)/shard_map/reshape;reshape | solution.py:66
  271.3 7.3 %fusion.7 = f32[1024,192]{0,1:T(8,128)} fusion(bf16[1024,4096]{1,0:T(8,128)(2,1)} %reshape_reshape.3, bf16[1,192,4096]{2,1,0:T(8,128)(2,1)S(1)} %copy-done), kind=kOutput, calls=%fused_computation.14 | convolution fusion | flops 1610612736 | bytes 10747904 | tf_op jit(solution)/shard_map/rd,fd->rf/dot_general | solution.py:71
  278.6 3.8 fusion.10
  282.4 11.3 %copy.60 = bf16[64,16,4096]{2,1,0:T(8,128)(2,1)} copy(bf16[64,16,4096]{2,0,1:T(8,128)(2,1)} %all-gather.3.cloned.1.call-done) | data formatting | bytes 16777216 | tf_op jit(solution)/shard_map/all_gather | solution.py:64
  293.8 0.0 copy-done.7
  293.8 6.4 %multiply_convert_fusion.1 = (bf16[1024,192]{0,1:T(8,128)(2,1)S(1)}, bf16[1024,192]{0,1:T(8,128)(2,1)S(1)}) fusion(f32[1024,192]{0,1:T(8,128)S(1)} %copy-done.8, f32[1024,192]{0,1:T(8,128)S(1)} %copy-done.10, bf16[1024,4096]{1,0:T(8,128)(2,1)} %bitcast.51, bf16[1,192,4096]{2,1,0:T(8,128)(2,1)S(1)} %copy-done.7), kind=kOutput, calls=%fused_computation.22 | convolution fusion | flops 1613168640 | bytes 12320768 | tf_op jit(solution)/shard_map/rd,fd->rf/dot_general | solution.py:76
  300.3 0.0 copy-start.4
  300.3 8.4 %fusion.5 = f32[1024,4096]{1,0:T(8,128)} fusion(bf16[1024,192]{0,1:T(8,128)(2,1)S(1)} %get-tuple-element.5, bf16[1,192,4096]{2,1,0:T(8,128)(2,1)S(1)} %copy-done), kind=kOutput, calls=%fused_computation.12 | convolution fusion | flops 1610612736 | bytes 18743296 | tf_op jit(solution)/shard_map/rf,fd->rd/dot_general | solution.py:90
  308.6 11.4 %add_convert_fusion = bf16[1024,4096]{1,0:T(8,128)(2,1)} fusion(f32[1024,4096]{1,0:T(8,128)} %fusion.5, bf16[1024,192]{0,1:T(8,128)(2,1)S(1)} %get-tuple-element.4, bf16[1,192,4096]{2,1,0:T(8,128)(2,1)S(1)} %copy-done.3), kind=kOutput, calls=%fused_computation | convolution fusion | flops 1619001344 | bytes 27131904 | tf_op jit(solution)/shard_map/rf,fd->rd/dot_general | solution.py:91
  320.0 13.1 %reshape.46 = bf16[64,4,4,4096]{3,2,1,0:T(4,128)(2,1)} reshape(bf16[1024,4096]{1,0:T(8,128)(2,1)} %add_convert_fusion) | data formatting | bytes 16777216 | tf_op jit(solution)/shard_map/reshape | solution.py:94
  333.1 11.2 %copy.64 = bf16[64,4,4,4096]{3,0,2,1:T(8,128)(2,1)} copy(bf16[64,4,4,4096]{3,2,1,0:T(4,128)(2,1)} %reshape.46) | data formatting | bytes 16777216 | tf_op jit(solution)/shard_map/optimization_barrier | solution.py:95
  344.3 0.0 reduce-scatter.2.cloned.1.call-update
  344.3 84.4 %reduce-scatter.2.cloned.1.call-done = bf16[64,1,4,4096]{3,0,2,1:T(8,128)(2,1)} async-done(((bf16[64,4,4,4096]{3,0,2,1:T(8,128)(2,1)}), bf16[64,1,4,4096]{3,0,2,1:T(8,128)(2,1)}) %reduce-scatter.2.cloned.1.call-update) | async-done | bytes 2097168 | tf_op jit(solution)/shard_map/reduce_scatter | solution.py:96
  428.7 4.6 copy.65
  433.3 11.3 %all-to-all-start.3 = ((bf16[64,4,4096]{2,1,0:T(4,128)(2,1)}), bf16[64,4,4096]{2,1,0:T(4,128)(2,1)}, u32[]{:S(2)}, u32[]{:S(2)}) async-start(bf16[64,4,4096]{2,1,0:T(4,128)(2,1)} %copy.65), calls=%async_computation.4 | async-start | bytes 4194304 | tf_op jit(solution)/shard_map/all_to_all | solution.py:99
  444.6 0.0 slice-start
  444.6 6.5 %fusion.1 = bf16[1,192,4096]{2,1,0:T(8,128)(2,1)} fusion(bf16[1024,192]{0,1:T(8,128)(2,1)S(1)} %copy-done.5, bf16[1024,4096]{1,0:T(8,128)(2,1)} %reshape_reshape.3), kind=kOutput, calls=%fused_computation.7 | convolution fusion | flops 1611399168 | bytes 10354688 | tf_op jit(solution)/shard_map/rf,rd->fd/dot_general | solution.py:87
  451.1 6.5 %fusion = bf16[1,192,4096]{2,1,0:T(8,128)(2,1)} fusion(bf16[1024,192]{0,1:T(8,128)(2,1)S(1)} %get-tuple-element.5, bf16[1024,4096]{1,0:T(8,128)(2,1)} %reshape_reshape.3), kind=kOutput, calls=%fused_computation.6 | convolution fusion | flops 1611399168 | bytes 10354688 | tf_op jit(solution)/shard_map/rf,rd->fd/dot_general | solution.py:84
  457.6 0.0 slice-done
  457.6 0.0 copy-done.9
  457.6 0.0 copy-start.1
  457.6 3.0 fusion.2
  460.6 35.0 %all-to-all-done.3 = bf16[64,4,4096]{2,1,0:T(4,128)(2,1)} async-done(((bf16[64,4,4096]{2,1,0:T(4,128)(2,1)}), bf16[64,4,4096]{2,1,0:T(4,128)(2,1)}, u32[]{:S(2)}, u32[]{:S(2)}) %all-to-all-start.3) | async-done | bytes 2097184 | tf_op jit(solution)/shard_map/all_to_all | solution.py:99
  495.6 4.6 fusion.3
  (25 shorter events, 0.1 us)
Async XLA Ops:
  7.2 264.1 %copy-start = (bf16[1,192,4096]{2,1,0:T(8,128)(2,1)S(1)}, bf16[1,192,4096]{2,1,0:T(8,128)(2,1)}, u32[]{:S(2)}) copy-start(bf16[1,192,4096]{2,1,0:T(8,128)(2,1)} %param.11) | copy-start | bytes 4718596
  7.2 275.3 %all-gather.3.cloned.1.call-start = ((), (), s32[]{:S(2)}) async-start(), calls=%async_computation.6 | async-start | bytes 10485760 | tf_op jit(solution)/shard_map/all_gather | solution.py:64
  80.7 0.9 copy-start.6
  80.7 348.0 %reduce-scatter.2.cloned.1.call-start = ((), (), s32[]{:S(2)}) async-start(), calls=%async_computation.5 | async-start | bytes 10485760 | tf_op jit(solution)/shard_map/reduce_scatter | solution.py:96
  271.3 7.3 %copy-start.2 = (bf16[1024,4096]{1,0:T(8,128)(2,1)S(1)}, bf16[1024,4096]{1,0:T(8,128)(2,1)}, u32[]{:S(2)}) copy-start(bf16[1024,4096]{1,0:T(8,128)(2,1)} %reshape_reshape.3) | copy-start | bytes 25165828
  271.3 7.3 %copy-start.3 = (bf16[1,192,4096]{2,1,0:T(8,128)(2,1)S(1)}, bf16[1,192,4096]{2,1,0:T(8,128)(2,1)}, u32[]{:S(2)}) copy-start(bf16[1,192,4096]{2,1,0:T(8,128)(2,1)} %param.12) | copy-start | bytes 4718596
  282.4 11.4 %copy-start.7 = (bf16[1,192,4096]{2,1,0:T(8,128)(2,1)S(1)}, bf16[1,192,4096]{2,1,0:T(8,128)(2,1)}, u32[]{:S(2)}) copy-start(bf16[1,192,4096]{2,1,0:T(8,128)(2,1)} %param.13) | copy-start | bytes 4718596
  282.4 11.4 %copy-start.8 = (f32[1024,192]{0,1:T(8,128)S(1)}, f32[1024,192]{0,1:T(8,128)}, u32[]{:S(2)}) copy-start(f32[1024,192]{0,1:T(8,128)} %fusion.7) | copy-start | bytes 2359300
  282.4 11.4 %copy-start.10 = (f32[1024,192]{0,1:T(8,128)S(1)}, f32[1024,192]{0,1:T(8,128)}, u32[]{:S(2)}) copy-start(f32[1024,192]{0,1:T(8,128)} %fusion.10) | copy-start | bytes 2359300
  300.3 8.4 %copy-start.4 = (bf16[1024,192]{0,1:T(8,128)(2,1)}, bf16[1024,192]{0,1:T(8,128)(2,1)S(1)}, u32[]{:S(2)}) copy-start(bf16[1024,192]{0,1:T(8,128)(2,1)S(1)} %get-tuple-element.4) | copy-start | bytes 1179652
  433.3 11.4 %copy-start.5 = (bf16[1024,192]{0,1:T(8,128)(2,1)S(1)}, bf16[1024,192]{0,1:T(8,128)(2,1)}, u32[]{:S(2)}) copy-start(bf16[1024,192]{0,1:T(8,128)(2,1)} %copy-done.4) | copy-start | bytes 1179652
  433.3 62.4 %all-to-all-start.3 = ((bf16[64,4,4096]{2,1,0:T(4,128)(2,1)}), bf16[64,4,4096]{2,1,0:T(4,128)(2,1)}, u32[]{:S(2)}, u32[]{:S(2)}) async-start(bf16[64,4,4096]{2,1,0:T(4,128)(2,1)} %copy.65), calls=%async_computation.4 | async-start | bytes 4194304 | tf_op jit(solution)/shard_map/all_to_all | solution.py:99
  444.6 13.0 %slice-start = ((s8[8388608]{0:T(1024)(128)(4,1)}), s8[4194304]{0:T(1024)(128)(4,1)S(1)}, s32[]{:S(2)}) async-start(s8[8388608]{0:T(1024)(128)(4,1)} %bitcast.52), calls=%async_computation.7 | async-start | bytes 8388608
  451.1 6.5 %slice-start.1 = ((s8[8388608]{0:T(1024)(128)(4,1)}), s8[4194304]{0:T(1024)(128)(4,1)S(1)}, s32[]{:S(2)}) async-start(s8[8388608]{0:T(1024)(128)(4,1)} %bitcast.52), calls=%async_computation.8 | async-start | bytes 8388608
  451.1 6.5 %copy-start.9 = (f32[1024,192]{0,1:T(8,128)S(1)}, f32[1024,192]{0,1:T(8,128)}, u32[]{:S(2)}) copy-start(f32[1024,192]{0,1:T(8,128)} %fusion.7) | copy-start | bytes 2359300
  451.1 6.5 %copy-start.11 = (f32[1024,192]{0,1:T(8,128)S(1)}, f32[1024,192]{0,1:T(8,128)}, u32[]{:S(2)}) copy-start(f32[1024,192]{0,1:T(8,128)} %fusion.10) | copy-start | bytes 2359300
  457.6 42.6 %copy-start.1 = (bf16[1,192,4096]{2,1,0:T(8,128)(2,1)S(1)}, bf16[1,192,4096]{2,1,0:T(8,128)(2,1)}, u32[]{:S(2)}) copy-start(bf16[1,192,4096]{2,1,0:T(8,128)(2,1)} %param.11) | copy-start | bytes 4718596
Sparse Core Ops, SparseCore 0:
  80.9 88.6 all-gather.2
  344.4 84.2 reduce-scatter.1
